TPU v7x, 32 devices: a whole 2x2x4 slice. The times are simulated.
32 devices in a mesh: dp: 8 (over z, y), tensor: 4 (over x, core).
Axes of the slice: x: 2, y: 2, z: 4, core: 2. Of those that a mesh axis runs over, the one named last changes fastest.
Arguments:
- tokens: bfloat16 [4096, 2048], P(('dp', 'tensor')), may hold values from -6 to 6
- lengths: int32 [8, 4], P('dp'), may hold values from 0 to 512, as said below
- w_query: bfloat16 [2048, 2048], P(None, 'tensor'), may hold values from -0.125 to 0.125
- w_key: bfloat16 [2048, 2048], P(None, 'tensor'), may hold values from -0.125 to 0.125
- w_value: bfloat16 [2048, 2048], P(None, 'tensor'), may hold values from -0.125 to 0.125
- w_out: bfloat16 [2048, 2048], P('tensor'), may hold values from -0.125 to 0.125
- w_gate: bfloat16 [2048, 8192], P(None, 'tensor'), may hold values from -0.125 to 0.125
- w_up: bfloat16 [2048, 8192], P(None, 'tensor'), may hold values from -0.125 to 0.125
- w_down: bfloat16 [8192, 2048], P('tensor'), may hold values from -0.0625 to 0.0625
- gain_query: float32 [2048], P('tensor'), may hold values from 0.1 to 1.9
- gain_key: float32 [2048], P('tensor'), may hold values from 0.1 to 1.9
- gain_attn: float32 [2048], replicated, may hold values from 0.1 to 1.9
- gain_mlp: float32 [2048], replicated, may hold values from 0.1 to 1.9
- cotangent: bfloat16 [4096, 2048], P(('dp', 'tensor')), may hold values from -6 to 6
Outputs:
- output: bfloat16 [4096, 2048], P(('dp', 'tensor'))
- grad_tokens: bfloat16 [4096, 2048], P(('dp', 'tensor'))
- grad_w_query: float32 [2048, 2048], P('dp', 'tensor')
- grad_w_key: float32 [2048, 2048], P('dp', 'tensor')
- grad_w_value: float32 [2048, 2048], P('dp', 'tensor')
- grad_w_out: float32 [2048, 2048], P('tensor', 'dp')
- grad_w_gate: float32 [2048, 8192], P('dp', 'tensor')
- grad_w_up: float32 [2048, 8192], P('dp', 'tensor')
- grad_w_down: float32 [8192, 2048], P('tensor', 'dp')
- grad_gain_query: float32 [2048], P('tensor')
- grad_gain_key: float32 [2048], P('tensor')
- grad_gain_attn: float32 [2048], replicated
- grad_gain_mlp: float32 [2048], replicated
Inputs may be any that keep to these rules, and one draw needn't show every extreme that they name: Each row lists the lengths of its sequences in order, then zeros; every nonzero length is 128 or more and they sum to 512; row 0 holds one sequence of 512 tokens.
All inputs are finite; a program needn't handle non-finite values.
Results may differ from a plain program's by a relative error of at most 0.023.
Values may be sent and summed in bfloat16 or wider, within the bound.
A program may use at most 256 MiB of HBM per device.

v0:
```python
import math
import jax
import jax.numpy as jnp
from jax import lax
from jax.sharding import PartitionSpec as P

HD = 128
ROW_LEN = 512
EPS = 1e-06
THETA = 500000.0


def rotate(values, offsets, rot_sign):
    half_width = values.shape[-1] // 2
    frequency = jnp.exp(
        jnp.arange(half_width, dtype=jnp.float32) * (-2.0 * math.log(THETA) / values.shape[-1])
    )
    angles = offsets.astype(jnp.float32)[..., None, None] * frequency
    cosines = jnp.cos(angles)
    sine_part = rot_sign * jnp.sin(angles)
    first_half = values[..., :half_width]
    second_half = values[..., half_width:]
    return jnp.concatenate(
        [
            first_half * cosines - second_half * sine_part,
            second_half * cosines + first_half * sine_part,
        ],
        axis=-1,
    )


def row_layout(lengths_row):
    seq_ends = jnp.cumsum(lengths_row)
    position = jnp.arange(ROW_LEN, dtype=jnp.int32)
    passed = (position[:, None] >= seq_ends[None, :]).astype(jnp.int32)
    segment = jnp.sum(passed, axis=1)
    seq_start = jnp.sum(passed * lengths_row[None, :], axis=1)
    return (segment, position - seq_start)


def allowed_mask(segment):
    position = jnp.arange(segment.shape[0], dtype=jnp.int32)
    return (segment[:, None] == segment[None, :]) & (position[None, :] <= position[:, None])


def times_t(left_mat, right_mat):
    return lax.dot_general(
        left_mat, right_mat, (((1,), (1,)), ((), ())), preferred_element_type=jnp.float32
    )


def t_times(left_mat, right_mat):
    return lax.dot_general(
        left_mat, right_mat, (((0,), (0,)), ((), ())), preferred_element_type=jnp.float32
    )


def masked_scores(queries_low, keys_low, segment):
    scale_factor = 1.0 / math.sqrt(queries_low.shape[-1])
    scores = (
        jnp.einsum("qhd,khd->hqk", queries_low, keys_low, preferred_element_type=jnp.float32)
        * scale_factor
    )
    return jnp.where(allowed_mask(segment)[None], scores, -1e30)


def attend(block_item):
    queries_low, keys_low, values_low, segment = block_item
    scores = masked_scores(queries_low, keys_low, segment)
    row_max = jnp.max(scores, axis=-1, keepdims=True)
    shifted = jnp.exp(scores - row_max)
    row_total = jnp.sum(shifted, axis=-1, keepdims=True)
    attn_weights = (shifted / row_total).astype(jnp.bfloat16)
    mixed = jnp.einsum("hqk,khd->qhd", attn_weights, values_low, preferred_element_type=jnp.float32)
    return (mixed.astype(jnp.bfloat16), (row_max + jnp.log(row_total))[..., 0])


def attend_back(block_item):
    queries_low, keys_low, values_low, segment, log_total, grad_mixed = block_item
    scale_factor = 1.0 / math.sqrt(queries_low.shape[-1])
    scores = masked_scores(queries_low, keys_low, segment)
    attn_weights = jnp.exp(scores - log_total[..., None])
    grad_weights = jnp.einsum(
        "qhd,khd->hqk", grad_mixed, values_low, preferred_element_type=jnp.float32
    )
    row_dots = jnp.sum(attn_weights * grad_weights, axis=-1, keepdims=True)
    grad_scores = (attn_weights * (grad_weights - row_dots)).astype(jnp.bfloat16)
    grad_queries = scale_factor * jnp.einsum(
        "hqk,khd->qhd", grad_scores, keys_low, preferred_element_type=jnp.float32
    )
    grad_keys = scale_factor * jnp.einsum(
        "hqk,qhd->khd", grad_scores, queries_low, preferred_element_type=jnp.float32
    )
    grad_values = jnp.einsum(
        "hqk,qhd->khd",
        attn_weights.astype(jnp.bfloat16),
        grad_mixed,
        preferred_element_type=jnp.float32,
    )
    return (grad_queries, grad_keys, grad_values.astype(jnp.bfloat16))


def post_norm_back(grad_in, unit_rows, inv_scale, gain_vec):
    scaled = grad_in * gain_vec
    mean_dots = jnp.mean(scaled * unit_rows, axis=-1, keepdims=True)
    return (inv_scale * (scaled - unit_rows * mean_dots), jnp.sum(grad_in * unit_rows, axis=0))


def body(
    tokens,
    lengths,
    w_query,
    w_key,
    w_value,
    w_out,
    w_gate,
    w_up,
    w_down,
    gain_query,
    gain_key,
    gain_attn,
    gain_mlp,
    cotangent,
):
    rows_dev = lengths.shape[0]
    model_width = w_query.shape[0]
    local_width = w_query.shape[1]
    head_count = local_width // HD
    gathered = lax.all_gather(tokens, "tensor", axis=0, tiled=True)
    row_count = gathered.shape[0]
    segment, offsets = jax.vmap(row_layout)(lengths)
    queries = jnp.dot(gathered, w_query, preferred_element_type=jnp.float32)
    keys_raw = jnp.dot(gathered, w_key, preferred_element_type=jnp.float32)
    values_low = jnp.dot(gathered, w_value, preferred_element_type=jnp.float32).astype(jnp.bfloat16)
    q_total, k_total = lax.psum(
        (jnp.sum(queries * queries, axis=1), jnp.sum(keys_raw * keys_raw, axis=1)), "tensor"
    )
    q_inv = lax.rsqrt(q_total / model_width + EPS)[:, None]
    k_inv = lax.rsqrt(k_total / model_width + EPS)[:, None]
    q_unit = queries * q_inv
    k_unit = keys_raw * k_inv

    def to_heads(values):
        return values.reshape(rows_dev, ROW_LEN, head_count, HD)

    queries_low = rotate(to_heads(q_unit * gain_query), offsets, 1.0).astype(jnp.bfloat16)
    keys_low = rotate(to_heads(k_unit * gain_key), offsets, 1.0).astype(jnp.bfloat16)
    values_heads = to_heads(values_low)
    mixed_heads, log_total = lax.map(attend, (queries_low, keys_low, values_heads, segment))
    mixed_low = mixed_heads.reshape(row_count, local_width)
    attn_out = lax.psum_scatter(
        jnp.dot(mixed_low, w_out, preferred_element_type=jnp.float32).astype(jnp.bfloat16),
        "tensor",
        scatter_dimension=0,
        tiled=True,
    ).astype(jnp.float32)
    a_inv = lax.rsqrt(jnp.mean(attn_out * attn_out, axis=1, keepdims=True) + EPS)
    a_unit = attn_out * a_inv
    hidden = tokens.astype(jnp.float32) + a_unit * gain_attn
    hidden_all = lax.all_gather(hidden.astype(jnp.bfloat16), "tensor", axis=0, tiled=True)
    gate_acts = jnp.dot(hidden_all, w_gate, preferred_element_type=jnp.float32)
    up_acts = jnp.dot(hidden_all, w_up, preferred_element_type=jnp.float32)
    gate_sigmoid = jax.nn.sigmoid(gate_acts)
    inner_low = (gate_acts * gate_sigmoid * up_acts).astype(jnp.bfloat16)
    mlp_out = lax.psum_scatter(
        jnp.dot(inner_low, w_down, preferred_element_type=jnp.float32).astype(jnp.bfloat16),
        "tensor",
        scatter_dimension=0,
        tiled=True,
    ).astype(jnp.float32)
    f_inv = lax.rsqrt(jnp.mean(mlp_out * mlp_out, axis=1, keepdims=True) + EPS)
    f_unit = mlp_out * f_inv
    output = (hidden + f_unit * gain_mlp).astype(jnp.bfloat16)
    grad_output = cotangent.astype(jnp.float32)
    grad_mlp, grad_gain_mlp_part = post_norm_back(grad_output, f_unit, f_inv, gain_mlp)
    mlp_grad_all = lax.all_gather(grad_mlp.astype(jnp.bfloat16), "tensor", axis=0, tiled=True)
    grad_w_down = t_times(inner_low, mlp_grad_all)
    grad_inner = times_t(mlp_grad_all, w_down)
    grad_gate_low = (
        grad_inner * up_acts * gate_sigmoid * (1.0 + gate_acts * (1.0 - gate_sigmoid))
    ).astype(jnp.bfloat16)
    grad_up_low = (grad_inner * gate_acts * gate_sigmoid).astype(jnp.bfloat16)
    grad_w_gate = t_times(hidden_all, grad_gate_low)
    grad_w_up = t_times(hidden_all, grad_up_low)
    grad_hidden = grad_output + lax.psum_scatter(
        (times_t(grad_gate_low, w_gate) + times_t(grad_up_low, w_up)).astype(jnp.bfloat16),
        "tensor",
        scatter_dimension=0,
        tiled=True,
    ).astype(jnp.float32)
    grad_attn, grad_gain_attn_part = post_norm_back(grad_hidden, a_unit, a_inv, gain_attn)
    attn_grad_all = lax.all_gather(grad_attn.astype(jnp.bfloat16), "tensor", axis=0, tiled=True)
    grad_w_out = t_times(mixed_low, attn_grad_all)
    grad_mixed = times_t(attn_grad_all, w_out).astype(jnp.bfloat16)
    grad_q_rot, grad_k_rot, grad_values_low = lax.map(
        attend_back, (queries_low, keys_low, values_heads, segment, log_total, to_heads(grad_mixed))
    )
    grad_q_norm = rotate(grad_q_rot, offsets, -1.0).reshape(row_count, local_width)
    grad_k_norm = rotate(grad_k_rot, offsets, -1.0).reshape(row_count, local_width)
    grad_gain_query_part = jnp.sum(grad_q_norm * q_unit, axis=0)
    grad_gain_key_part = jnp.sum(grad_k_norm * k_unit, axis=0)
    q_scaled = grad_q_norm * gain_query
    k_scaled = grad_k_norm * gain_key
    q_dots, k_dots = lax.psum(
        (jnp.sum(q_scaled * q_unit, axis=1), jnp.sum(k_scaled * k_unit, axis=1)), "tensor"
    )
    grad_queries_low = (q_inv * (q_scaled - q_unit * (q_dots / model_width)[:, None])).astype(
        jnp.bfloat16
    )
    grad_keys_low = (k_inv * (k_scaled - k_unit * (k_dots / model_width)[:, None])).astype(
        jnp.bfloat16
    )
    grad_values_flat = grad_values_low.reshape(row_count, local_width)
    grad_w_query = t_times(gathered, grad_queries_low)
    grad_w_key = t_times(gathered, grad_keys_low)
    grad_w_value = t_times(gathered, grad_values_flat)
    grad_tokens = (
        grad_hidden
        + lax.psum_scatter(
            (
                times_t(grad_queries_low, w_query)
                + times_t(grad_keys_low, w_key)
                + times_t(grad_values_flat, w_value)
            ).astype(jnp.bfloat16),
            "tensor",
            scatter_dimension=0,
            tiled=True,
        ).astype(jnp.float32)
    ).astype(jnp.bfloat16)
    tensor_start = lax.axis_index("tensor") * local_width
    zero_row = jnp.zeros((model_width,), jnp.float32)
    q_full = lax.dynamic_update_slice(zero_row, grad_gain_query_part, (tensor_start,))
    k_full = lax.dynamic_update_slice(zero_row, grad_gain_key_part, (tensor_start,))
    gain_stack = jnp.stack([q_full, k_full, grad_gain_attn_part, grad_gain_mlp_part])
    gain_total = lax.psum(gain_stack, ("dp", "tensor"))
    grad_gain_query = lax.dynamic_slice(gain_total[0], (tensor_start,), (local_width,))
    grad_gain_key = lax.dynamic_slice(gain_total[1], (tensor_start,), (local_width,))
    summed = (
        lax.psum_scatter(
            grad_w_query.astype(jnp.bfloat16), "dp", scatter_dimension=0, tiled=True
        ).astype(jnp.float32),
        lax.psum_scatter(
            grad_w_key.astype(jnp.bfloat16), "dp", scatter_dimension=0, tiled=True
        ).astype(jnp.float32),
        lax.psum_scatter(
            grad_w_value.astype(jnp.bfloat16), "dp", scatter_dimension=0, tiled=True
        ).astype(jnp.float32),
        lax.psum_scatter(
            grad_w_out.astype(jnp.bfloat16), "dp", scatter_dimension=1, tiled=True
        ).astype(jnp.float32),
        lax.psum_scatter(
            grad_w_gate.astype(jnp.bfloat16), "dp", scatter_dimension=0, tiled=True
        ).astype(jnp.float32),
        lax.psum_scatter(
            grad_w_up.astype(jnp.bfloat16), "dp", scatter_dimension=0, tiled=True
        ).astype(jnp.float32),
        lax.psum_scatter(
            grad_w_down.astype(jnp.bfloat16), "dp", scatter_dimension=1, tiled=True
        ).astype(jnp.float32),
    )
    return (
        output,
        grad_tokens,
        summed[0],
        summed[1],
        summed[2],
        summed[3],
        summed[4],
        summed[5],
        summed[6],
        grad_gain_query,
        grad_gain_key,
        gain_total[2],
        gain_total[3],
    )


def solution(mesh):
    placed = (
        P(("dp", "tensor"), None),
        P("dp", None),
        P(None, "tensor"),
        P(None, "tensor"),
        P(None, "tensor"),
        P("tensor", None),
        P(None, "tensor"),
        P(None, "tensor"),
        P("tensor", None),
        P("tensor"),
        P("tensor"),
        P(),
        P(),
        P(("dp", "tensor"), None),
    )
    return jax.shard_map(
        body,
        mesh=mesh,
        in_specs=placed,
        out_specs=(
            P(("dp", "tensor"), None),
            P(("dp", "tensor"), None),
            P("dp", "tensor"),
            P("dp", "tensor"),
            P("dp", "tensor"),
            P("tensor", "dp"),
            P("dp", "tensor"),
            P("dp", "tensor"),
            P("tensor", "dp"),
            P("tensor"),
            P("tensor"),
            P(),
            P(),
        ),
        check_vma=False,
    )
```

profile of v0, /device:TPU:0, one launch (start us, length us, event | category | flops | bytes accessed | tf_op | source)
XLA Modules:
  0.0 1118.6 jit_solution(15427189430564919261)
XLA Ops:
  12.3 22.6 %all-gather.5.cloned.1.call-done = bf16[512,2048]{1,0:T(8,128)(2,1)} async-done(((bf16[128,2048]{1,0:T(8,128)(2,1)}), bf16[512,2048]{1,0:T(8,128)(2,1)}) %all-gather.5.cloned.1.call-update) | async-done | bytes 2097168 | tf_op jit(solution)/shard_map/all_gather | solution.py:129
  34.9 4.0 multiply_reduce_fusion.4
  38.9 2.3 multiply_reduce_fusion.3
  41.2 5.9 all-reduce.1
  55.3 2.8 fusion.41
  60.3 2.5 copy-done.19
  66.5 2.6 convolution_convert_fusion.8
  69.2 32.6 %reduce-scatter.12.cloned.1.call-done = bf16[128,2048]{1,0:T(8,128)(2,1)} async-done(((bf16[512,2048]{1,0:T(8,128)(2,1)}), bf16[128,2048]{1,0:T(8,128)(2,1)}) %reduce-scatter.12.cloned.1.call-update) | async-done | bytes 524304 | tf_op jit(solution)/shard_map/reduce_scatter | solution.py:151
  103.0 2.1 fusion.40
  105.4 22.5 %all-gather.7.cloned.1.call-done = bf16[512,2048]{1,0:T(8,128)(2,1)} async-done(((bf16[128,2048]{1,0:T(8,128)(2,1)}), bf16[512,2048]{1,0:T(8,128)(2,1)}) %all-gather.7.cloned.1.call-update) | async-done | bytes 2097168 | tf_op jit(solution)/shard_map/all_gather | solution.py:160
  127.9 8.5 fusion.52
  136.4 11.7 %multiply_convert_fusion.3 = (bf16[512,2048]{1,0:T(8,128)(2,1)S(1)}, f32[512,2048]{1,0:T(8,128)}) fusion(f32[512,2048]{1,0:T(8,128)S(1)} %fusion.52, bf16[512,2048]{1,0:T(8,128)(2,1)S(1)} %copy-done.40, bf16[2048,2048]{1,0:T(8,128)(2,1)} %param.21), kind=kOutput, calls=%fused_computation.10 | convolution fusion | flops 4301258752 | bytes 20971520 | tf_op jit(solution)/shard_map/dot_general | solution.py:162
  149.5 5.7 convolution_convert_fusion.7
  155.3 31.5 %reduce-scatter.14.cloned.1.call-done = bf16[128,2048]{1,0:T(8,128)(2,1)} async-done(((bf16[512,2048]{1,0:T(8,128)(2,1)}), bf16[128,2048]{1,0:T(8,128)(2,1)}) %reduce-scatter.14.cloned.1.call-update) | async-done | bytes 524304 | tf_op jit(solution)/shard_map/reduce_scatter | solution.py:165
  189.5 2.2 fusion.24
  192.2 22.3 %all-gather.9.cloned.1.call-done = bf16[512,2048]{1,0:T(8,128)(2,1)} async-done(((bf16[128,2048]{1,0:T(8,128)(2,1)}), bf16[512,2048]{1,0:T(8,128)(2,1)}) %all-gather.9.cloned.1.call-update) | async-done | bytes 2097168 | tf_op jit(solution)/shard_map/all_gather | solution.py:176
  214.5 11.9 %multiply_convert_fusion.1 = (bf16[512,2048]{1,0:T(8,128)(2,1)S(1)}, bf16[512,2048]{1,0:T(8,128)(2,1)S(1)}) fusion(f32[512,2048]{1,0:T(8,128)} %copy-done.42, f32[512,2048]{1,0:T(8,128)} %get-tuple-element.138, bf16[512,2048]{1,0:T(8,128)(2,1)} %all-gather.9.cloned.1.call-done, bf16[2048,2048]{1,0:T(8,128)(2,1)} %param.22), kind=kOutput, calls=%fused_computation.8 | convolution fusion | flops 4308598784 | bytes 23068672 | tf_op jit(solution)/shard_map/dot_general | solution.py:47
  226.4 8.5 fusion.53
  234.9 9.2 add_convert_fusion.1
  244.2 31.6 %reduce-scatter.16.cloned.1.call-done = bf16[128,2048]{1,0:T(8,128)(2,1)} async-done(((bf16[512,2048]{1,0:T(8,128)(2,1)}), bf16[128,2048]{1,0:T(8,128)(2,1)}) %reduce-scatter.16.cloned.1.call-update) | async-done | bytes 524304 | tf_op jit(solution)/shard_map/reduce_scatter | solution.py:185
  277.3 2.9 fusion.29
  280.5 22.5 %all-gather.11.cloned.1.call-done = bf16[512,2048]{1,0:T(8,128)(2,1)} async-done(((bf16[128,2048]{1,0:T(8,128)(2,1)}), bf16[512,2048]{1,0:T(8,128)(2,1)}) %all-gather.11.cloned.1.call-update) | async-done | bytes 2097168 | tf_op jit(solution)/shard_map/all_gather | solution.py:192
  303.0 3.6 convolution_convert_fusion.9
  314.5 2.6 copy.56
  317.1 2.0 fusion.38
  320.6 2.5 copy.60
  325.0 5.9 all-reduce
  333.1 2.6 fusion.2
  338.5 2.6 fusion.3
  341.1 3.3 fusion.18
  345.3 2.6 fusion.4
  348.2 4.3 convolution_convert_fusion.3
  356.1 2.6 add_convert_fusion
  358.8 10.0 convolution_convert_fusion.2
  369.1 10.1 convolution_convert_fusion.1
  379.3 10.0 convolution_convert_fusion
  389.5 40.7 %psum.39 = f32[4,2048]{1,0:T(4,128)S(1)} all-reduce(f32[4,2048]{1,0:T(4,128)S(1)} %pad_maximum_fusion.8), channel_id=1, replica_groups=mesh['dp'=8,'tensor'=4] {'dp','tensor'}, use_global_device_ids=true, to_apply=%region_33.34 | all-reduce | flops 8192 | bytes 65536 | tf_op jit(solution)/shard_map/psum | solution.py:235
  433.8 43.0 %reduce-scatter.22.cloned.1.call-done = bf16[256,512]{0,1:T(8,128)(2,1)} async-done(((bf16[2048,512]{0,1:T(8,128)(2,1)}), bf16[256,512]{0,1:T(8,128)(2,1)}) %reduce-scatter.22.cloned.1.call-update) | async-done | bytes 262160 | tf_op jit(solution)/shard_map/reduce_scatter | solution.py:242
  478.8 69.0 %reduce-scatter.24.cloned.1.call-done = bf16[256,512]{0,1:T(8,128)(2,1)} async-done(((bf16[2048,512]{0,1:T(8,128)(2,1)}), bf16[256,512]{0,1:T(8,128)(2,1)}) %reduce-scatter.24.cloned.1.call-update) | async-done | bytes 262160 | tf_op jit(solution)/shard_map/reduce_scatter | solution.py:245
  549.6 69.2 %reduce-scatter.26.cloned.1.call-done = bf16[512,256]{1,0:T(8,128)(2,1)} async-done(((bf16[512,2048]{1,0:T(8,128)(2,1)}), bf16[512,256]{1,0:T(8,128)(2,1)}) %reduce-scatter.26.cloned.1.call-update) | async-done | bytes 262160 | tf_op jit(solution)/shard_map/reduce_scatter | solution.py:248
  620.6 31.8 %reduce-scatter.18.cloned.1.call-done = bf16[128,2048]{1,0:T(8,128)(2,1)} async-done(((bf16[512,2048]{1,0:T(8,128)(2,1)}), bf16[128,2048]{1,0:T(8,128)(2,1)}) %reduce-scatter.18.cloned.1.call-update) | async-done | bytes 524304 | tf_op jit(solution)/shard_map/reduce_scatter | solution.py:219
  652.4 2.1 add_convert_fusion.2
  654.4 150.6 %reduce-scatter.28.cloned.1.call-done = bf16[256,2048]{1,0:T(8,128)(2,1)} async-done(((bf16[2048,2048]{1,0:T(8,128)(2,1)}), bf16[256,2048]{1,0:T(8,128)(2,1)}) %reduce-scatter.28.cloned.1.call-update) | async-done | bytes 1048592 | tf_op jit(solution)/shard_map/reduce_scatter | solution.py:251
  805.0 2.8 convert_element_type.217
  807.8 149.2 %reduce-scatter.30.cloned.1.call-done = bf16[256,2048]{1,0:T(8,128)(2,1)} async-done(((bf16[2048,2048]{1,0:T(8,128)(2,1)}), bf16[256,2048]{1,0:T(8,128)(2,1)}) %reduce-scatter.30.cloned.1.call-update) | async-done | bytes 1048592 | tf_op jit(solution)/shard_map/reduce_scatter | solution.py:254
  957.0 2.8 convert_element_type.219
  959.8 149.1 %reduce-scatter.32.cloned.1.call-done = bf16[2048,256]{1,0:T(8,128)(2,1)} async-done(((bf16[2048,2048]{1,0:T(8,128)(2,1)}), bf16[2048,256]{1,0:T(8,128)(2,1)}) %reduce-scatter.32.cloned.1.call-update) | async-done | bytes 1048592 | tf_op jit(solution)/shard_map/reduce_scatter | solution.py:257
  1108.9 2.7 convert_element_type.221
  (181 shorter events, 57.4 us)
Async XLA Ops:
  7.2 27.7 %copy-start = (bf16[2048,512]{1,0:T(8,128)(2,1)S(1)}, bf16[2048,512]{1,0:T(8,128)(2,1)}, u32[]{:S(2)}) copy-start(bf16[2048,512]{1,0:T(8,128)(2,1)} %param.16) | copy-start | bytes 6291460
  7.2 27.7 %all-gather.5.cloned.1.call-start = ((), (), s32[]{:S(2)}) async-start(), calls=%async_computation.11 | async-start | bytes 2621440 | tf_op jit(solution)/shard_map/all_gather | solution.py:129
  7.9 93.8 %reduce-scatter.12.cloned.1.call-start = ((), (), s32[]{:S(2)}) async-start(), calls=%async_computation.12 | async-start | bytes 2621440 | tf_op jit(solution)/shard_map/reduce_scatter | solution.py:151
  34.9 4.0 copy-start.24
  34.9 4.0 copy-start.35
  38.9 8.1 copy-start.32
  48.5 2.7 copy-start.33
  55.3 2.9 copy-start.26
  58.2 1.4 copy-start.7
  59.6 5.1 copy-start.1
  59.6 3.1 copy-start.19
  59.7 3.7 copy-start.36
  64.7 1.8 copy-start.34
  69.1 33.9 %copy-start.5 = (bf16[128,2048]{1,0:T(8,128)(2,1)S(1)}, bf16[128,2048]{1,0:T(8,128)(2,1)}, u32[]{:S(2)}) copy-start(bf16[128,2048]{1,0:T(8,128)(2,1)} %param.14) | copy-start | bytes 1572868
  69.1 33.9 %copy-start.30 = (f32[2048]{0:T(1024)S(1)}, f32[2048]{0:T(1024)}, u32[]{:S(2)}) copy-start(f32[2048]{0:T(1024)} %param.25) | copy-start | bytes 24580
  69.1 58.8 %all-gather.7.cloned.1.call-start = ((), (), s32[]{:S(2)}) async-start(), calls=%async_computation.13 | async-start | bytes 2621440 | tf_op jit(solution)/shard_map/all_gather | solution.py:160
  105.1 81.7 %reduce-scatter.14.cloned.1.call-start = ((), (), s32[]{:S(2)}) async-start(), calls=%async_computation.14 | async-start | bytes 2621440 | tf_op jit(solution)/shard_map/reduce_scatter | solution.py:165
  127.9 8.5 copy-start.40
  127.9 21.6 %slice-start = ((s8[8388608]{0:T(1024)(128)(4,1)}), s8[4194304]{0:T(1024)(128)(4,1)S(1)}, s32[]{:S(2)}) async-start(s8[8388608]{0:T(1024)(128)(4,1)} %bitcast.128), calls=%async_computation.26 | async-start | bytes 8388608
  136.4 11.7 %copy-start.42 = (f32[512,2048]{1,0:T(8,128)}, f32[512,2048]{1,0:T(8,128)S(1)}, u32[]{:S(2)}) copy-start(f32[512,2048]{1,0:T(8,128)S(1)} %fusion.52) | copy-start | bytes 12582916
  136.4 13.1 %slice-start.1 = ((s8[8388608]{0:T(1024)(128)(4,1)}), s8[4194304]{0:T(1024)(128)(4,1)S(1)}, s32[]{:S(2)}) async-start(s8[8388608]{0:T(1024)(128)(4,1)} %bitcast.128), calls=%async_computation.27 | async-start | bytes 8388608
  155.2 32.9 %copy-start.3 = (bf16[128,2048]{1,0:T(8,128)(2,1)S(1)}, bf16[128,2048]{1,0:T(8,128)(2,1)}, u32[]{:S(2)}) copy-start(bf16[128,2048]{1,0:T(8,128)(2,1)} %param.27) | copy-start | bytes 1572868
  155.2 32.9 %copy-start.31 = (f32[2048]{0:T(1024)S(1)}, f32[2048]{0:T(1024)}, u32[]{:S(2)}) copy-start(f32[2048]{0:T(1024)} %param.26) | copy-start | bytes 24580
  155.2 59.3 %all-gather.9.cloned.1.call-start = ((), (), s32[]{:S(2)}) async-start(), calls=%async_computation.15 | async-start | bytes 2621440 | tf_op jit(solution)/shard_map/all_gather | solution.py:176
  191.8 84.0 %reduce-scatter.16.cloned.1.call-start = ((), (), s32[]{:S(2)}) async-start(), calls=%async_computation.16 | async-start | bytes 2621440 | tf_op jit(solution)/shard_map/reduce_scatter | solution.py:185
  226.4 8.5 copy-start.45
  226.4 8.5 copy-start.44
  244.1 31.6 %copy-start.4 = (bf16[128,2048]{1,0:T(8,128)(2,1)S(1)}, bf16[128,2048]{1,0:T(8,128)(2,1)}, u32[]{:S(2)}) copy-start(bf16[128,2048]{1,0:T(8,128)(2,1)} %reduce-scatter.12.cloned.1.call-done) | copy-start | bytes 1572868
  244.1 58.8 %all-gather.11.cloned.1.call-start = ((), (), s32[]{:S(2)}) async-start(), calls=%async_computation.17 | async-start | bytes 2621440 | tf_op jit(solution)/shard_map/all_gather | solution.py:192
  280.2 151.7 %reduce-scatter.20.cloned.1.call-start = ((), (), s32[]{:S(2)}) async-start(), calls=%async_computation.19 | async-start | bytes 2359296 | tf_op jit(solution)/shard_map/reduce_scatter | solution.py:239
  280.5 26.2 %copy-start.29 = (bf16[512,512]{0,1:T(8,128)(2,1)S(1)}, bf16[512,512]{0,1:T(8,128)(2,1)}, u32[]{:S(2)}) copy-start(bf16[512,512]{0,1:T(8,128)(2,1)} %copy-done.28) | copy-start | bytes 1572868
  303.0 3.7 copy-start.2
  317.1 2.0 copy-start.15
  317.1 2.2 copy-start.16
  330.9 2.2 copy-start.37
  335.7 141.2 %reduce-scatter.22.cloned.1.call-start = ((), (), s32[]{:S(2)}) async-start(), calls=%async_computation.20 | async-start | bytes 2359296 | tf_op jit(solution)/shard_map/reduce_scatter | solution.py:242
  335.7 2.7 copy-start.38
  341.1 206.7 %reduce-scatter.24.cloned.1.call-start = ((), (), s32[]{:S(2)}) async-start(), calls=%async_computation.21 | async-start | bytes 2359296 | tf_op jit(solution)/shard_map/reduce_scatter | solution.py:245
  341.1 4.2 copy-start.39
  347.9 270.9 %reduce-scatter.26.cloned.1.call-start = ((), (), s32[]{:S(2)}) async-start(), calls=%async_computation.22 | async-start | bytes 2359296 | tf_op jit(solution)/shard_map/reduce_scatter | solution.py:248
  352.5 299.8 %reduce-scatter.18.cloned.1.call-start = ((), (), s32[]{:S(2)}) async-start(), calls=%async_computation.18 | async-start | bytes 2621440 | tf_op jit(solution)/shard_map/reduce_scatter | solution.py:219
  352.6 1.8 copy-start.25
  354.4 1.6 copy-start.20
  354.4 1.7 copy-start.23
  358.7 446.3 %reduce-scatter.28.cloned.1.call-start = ((), (), s32[]{:S(2)}) async-start(), calls=%async_computation.23 | async-start | bytes 9437184 | tf_op jit(solution)/shard_map/reduce_scatter | solution.py:251
  368.8 588.2 %reduce-scatter.30.cloned.1.call-start = ((), (), s32[]{:S(2)}) async-start(), calls=%async_computation.24 | async-start | bytes 9437184 | tf_op jit(solution)/shard_map/reduce_scatter | solution.py:254
  379.2 729.7 %reduce-scatter.32.cloned.1.call-start = ((), (), s32[]{:S(2)}) async-start(), calls=%async_computation.25 | async-start | bytes 9437184 | tf_op jit(solution)/shard_map/reduce_scatter | solution.py:257
  389.3 263.0 %copy-start.6 = (bf16[128,2048]{1,0:T(8,128)(2,1)S(1)}, bf16[128,2048]{1,0:T(8,128)(2,1)}, u32[]{:S(2)}) copy-start(bf16[128,2048]{1,0:T(8,128)(2,1)} %reduce-scatter.16.cloned.1.call-done) | copy-start | bytes 1572868
  (15 other events, 17.1 us)
Sparse Core Ops, SparseCore 0:
  9.6 25.2 all-gather.4
  69.2 32.4 reduce-scatter.11
  105.3 22.5 all-gather.6
  155.3 31.4 reduce-scatter.13
  191.9 22.5 all-gather.8
  244.3 31.4 reduce-scatter.15
  280.4 22.5 all-gather.10
  335.8 69.3 reduce-scatter.19
  409.7 67.1 reduce-scatter.21
  480.7 67.0 reduce-scatter.23
  551.7 67.0 reduce-scatter.25
  621.9 30.3 reduce-scatter.17
  656.0 149.0 reduce-scatter.27
  808.9 148.0 reduce-scatter.29
  960.5 148.3 reduce-scatter.31
where the time goes:
time: 1130 us; the launch traced here: 1120 us
  waiting for transfers between devices  848 us (75%)
  matrix products  125 us (11%)
  blocking collectives  52.4 us (5%)
  other arithmetic  48.9 us (4%)
  local copies, waits for them, and re-layouts  26.8 us (2%)
  between operations  15 us (1%)
    reduce_scatter x1, waiting for transfers between devices, body(): lax.psum_scatter(grad_w_gate.astype(jnp.bfloat16), 'dp', scatter_dimensio...  151 us
    reduce_scatter x1, waiting for transfers between devices, body(): lax.psum_scatter(grad_w_up.astype(jnp.bfloat16), 'dp', scatter_dimension=...  149 us
    reduce_scatter x1, waiting for transfers between devices, body(): lax.psum_scatter(grad_w_down.astype(jnp.bfloat16), 'dp', scatter_dimensio...  149 us
    reduce_scatter x1, waiting for transfers between devices, body(): lax.psum_scatter(grad_w_out.astype(jnp.bfloat16), 'dp', scatter_dimension...  69.2 us
    reduce_scatter x1, waiting for transfers between devices, body(): lax.psum_scatter(grad_w_value.astype(jnp.bfloat16), 'dp', scatter_dimensi...  69 us
    reduce_scatter x1, waiting for transfers between devices, body(): lax.psum_scatter(grad_w_key.astype(jnp.bfloat16), 'dp', scatter_dimension...  43 us
    dot_general x7, matrix products, t_times(): lax.dot_general(left_mat, right_mat, (((0,), (0,)), ((), ())), preferred_...  42.3 us
    psum x1, blocking collectives, body(): gain_total = lax.psum(gain_stack, ('dp', 'tensor'))  40.7 us
  transfers between devices with their start and end apart: 15, of which 14 were waited for; matrix products, arithmetic and copies ran while one was open for 6% of the time, Pallas kernels for 0%

commit v1 on v0

--- a/solution.py
+++ b/solution.py
@@ -232,7 +232,7 @@
     q_full = lax.dynamic_update_slice(zero_row, grad_gain_query_part, (tensor_start,))
     k_full = lax.dynamic_update_slice(zero_row, grad_gain_key_part, (tensor_start,))
     gain_stack = jnp.stack([q_full, k_full, grad_gain_attn_part, grad_gain_mlp_part])
-    gain_total = lax.psum(gain_stack, ("dp", "tensor"))
+    gain_total = jnp.sum(lax.all_gather(gain_stack, ("dp", "tensor")), axis=0)
     grad_gain_query = lax.dynamic_slice(gain_total[0], (tensor_start,), (local_width,))
     grad_gain_key = lax.dynamic_slice(gain_total[1], (tensor_start,), (local_width,))
     summed = (

time: 1130 us -> 1170 us (1.035)
  waiting for transfers between devices: 848 us -> 934 us
  blocking collectives: 52.4 us -> 11.7 us
    reduce_scatter x1, waiting for transfers between devices: 0.01 us -> 58.1 us  [body(): lax.psum_scatter(grad_w_query.astype(jnp.bfloat16), 'dp', scatter_dimensi...]
    psum x1 -> x0, blocking collectives: 40.7 us -> none  [body(): gain_total = lax.psum(gain_stack, ('dp', 'tensor'))]
    reduce_scatter x1, waiting for transfers between devices: 43 us -> 69.8 us  [body(): lax.psum_scatter(grad_w_key.astype(jnp.bfloat16), 'dp', scatter_dimension...]
  transfers between devices with their start and end apart: 15 -> 16, of which waited for: 14 -> 15; matrix products, arithmetic and copies ran while one was open for 6% -> 7% of each run, Pallas kernels for 0% -> 0%
where the time goes in v1:
time: 1170 us
  waiting for transfers between devices  934 us (80%)
  matrix products  125 us (11%)
  other arithmetic  51 us (4%)
  local copies, waits for them, and re-layouts  26.8 us (2%)
  between operations  15.1 us (1%)
    reduce_scatter x1, waiting for transfers between devices, body(): lax.psum_scatter(grad_w_gate.astype(jnp.bfloat16), 'dp', scatter_dimensio...  150 us
    reduce_scatter x1, waiting for transfers between devices, body(): lax.psum_scatter(grad_w_down.astype(jnp.bfloat16), 'dp', scatter_dimensio...  149 us
    reduce_scatter x1, waiting for transfers between devices, body(): lax.psum_scatter(grad_w_up.astype(jnp.bfloat16), 'dp', scatter_dimension=...  149 us
    reduce_scatter x1, waiting for transfers between devices, body(): lax.psum_scatter(grad_w_key.astype(jnp.bfloat16), 'dp', scatter_dimension...  69.8 us
    reduce_scatter x1, waiting for transfers between devices, body(): lax.psum_scatter(grad_w_value.astype(jnp.bfloat16), 'dp', scatter_dimensi...  69.4 us
    reduce_scatter x1, waiting for transfers between devices, body(): lax.psum_scatter(grad_w_out.astype(jnp.bfloat16), 'dp', scatter_dimension...  69.1 us
    reduce_scatter x1, waiting for transfers between devices, body(): lax.psum_scatter(grad_w_query.astype(jnp.bfloat16), 'dp', scatter_dimensi...  58.1 us
    dot_general x7, matrix products, t_times(): lax.dot_general(left_mat, right_mat, (((0,), (0,)), ((), ())), preferred_...  42.2 us
  transfers between devices with their start and end apart: 16, of which 15 were waited for; matrix products, arithmetic and copies ran while one was open for 7% of the time, Pallas kernels for 0%

profile of v1, /device:TPU:0, one launch (start us, length us, event | category | flops | bytes accessed | tf_op | source)
XLA Modules:
  0.0 1165.3 jit_solution(8825576092158362530)
XLA Ops:
  12.3 22.6 %all-gather.8.cloned.1.call-done = bf16[512,2048]{1,0:T(8,128)(2,1)} async-done(((bf16[128,2048]{1,0:T(8,128)(2,1)}), bf16[512,2048]{1,0:T(8,128)(2,1)}) %all-gather.8.cloned.1.call-update) | async-done | bytes 2097168 | tf_op jit(solution)/shard_map/all_gather | solution.py:129
  34.9 4.0 multiply_reduce_fusion.4
  38.9 2.3 multiply_reduce_fusion.3
  41.2 5.9 all-reduce.1
  55.3 2.8 fusion.41
  60.2 2.5 copy-done.19
  66.5 2.6 convolution_convert_fusion.8
  69.2 32.6 %reduce-scatter.12.cloned.1.call-done = bf16[128,2048]{1,0:T(8,128)(2,1)} async-done(((bf16[512,2048]{1,0:T(8,128)(2,1)}), bf16[128,2048]{1,0:T(8,128)(2,1)}) %reduce-scatter.12.cloned.1.call-update) | async-done | bytes 524304 | tf_op jit(solution)/shard_map/reduce_scatter | solution.py:151
  103.0 2.1 fusion.40
  105.4 22.5 %all-gather.10.cloned.1.call-done = bf16[512,2048]{1,0:T(8,128)(2,1)} async-done(((bf16[128,2048]{1,0:T(8,128)(2,1)}), bf16[512,2048]{1,0:T(8,128)(2,1)}) %all-gather.10.cloned.1.call-update) | async-done | bytes 2097168 | tf_op jit(solution)/shard_map/all_gather | solution.py:160
  127.9 8.5 fusion.52
  136.4 11.7 %multiply_convert_fusion.3 = (bf16[512,2048]{1,0:T(8,128)(2,1)S(1)}, f32[512,2048]{1,0:T(8,128)}) fusion(f32[512,2048]{1,0:T(8,128)S(1)} %fusion.52, bf16[512,2048]{1,0:T(8,128)(2,1)S(1)} %copy-done.40, bf16[2048,2048]{1,0:T(8,128)(2,1)} %param.21), kind=kOutput, calls=%fused_computation.10 | convolution fusion | flops 4301258752 | bytes 20971520 | tf_op jit(solution)/shard_map/dot_general | solution.py:162
  149.5 5.7 convolution_convert_fusion.7
  155.3 31.5 %reduce-scatter.14.cloned.1.call-done = bf16[128,2048]{1,0:T(8,128)(2,1)} async-done(((bf16[512,2048]{1,0:T(8,128)(2,1)}), bf16[128,2048]{1,0:T(8,128)(2,1)}) %reduce-scatter.14.cloned.1.call-update) | async-done | bytes 524304 | tf_op jit(solution)/shard_map/reduce_scatter | solution.py:165
  189.5 2.2 fusion.24
  192.2 22.3 %all-gather.12.cloned.1.call-done = bf16[512,2048]{1,0:T(8,128)(2,1)} async-done(((bf16[128,2048]{1,0:T(8,128)(2,1)}), bf16[512,2048]{1,0:T(8,128)(2,1)}) %all-gather.12.cloned.1.call-update) | async-done | bytes 2097168 | tf_op jit(solution)/shard_map/all_gather | solution.py:176
  214.5 11.9 %multiply_convert_fusion.1 = (bf16[512,2048]{1,0:T(8,128)(2,1)S(1)}, bf16[512,2048]{1,0:T(8,128)(2,1)S(1)}) fusion(f32[512,2048]{1,0:T(8,128)} %copy-done.42, f32[512,2048]{1,0:T(8,128)} %get-tuple-element.151, bf16[512,2048]{1,0:T(8,128)(2,1)} %all-gather.12.cloned.1.call-done, bf16[2048,2048]{1,0:T(8,128)(2,1)} %param.22), kind=kOutput, calls=%fused_computation.8 | convolution fusion | flops 4308598784 | bytes 23068672 | tf_op jit(solution)/shard_map/dot_general | solution.py:47
  226.5 8.5 fusion.53
  234.9 9.2 add_convert_fusion.1
  244.2 31.6 %reduce-scatter.16.cloned.1.call-done = bf16[128,2048]{1,0:T(8,128)(2,1)} async-done(((bf16[512,2048]{1,0:T(8,128)(2,1)}), bf16[128,2048]{1,0:T(8,128)(2,1)}) %reduce-scatter.16.cloned.1.call-update) | async-done | bytes 524304 | tf_op jit(solution)/shard_map/reduce_scatter | solution.py:185
  277.3 2.9 fusion.29
  280.5 22.5 %all-gather.14.cloned.1.call-done = bf16[512,2048]{1,0:T(8,128)(2,1)} async-done(((bf16[128,2048]{1,0:T(8,128)(2,1)}), bf16[512,2048]{1,0:T(8,128)(2,1)}) %all-gather.14.cloned.1.call-update) | async-done | bytes 2097168 | tf_op jit(solution)/shard_map/all_gather | solution.py:192
  303.0 3.6 convolution_convert_fusion.9
  311.2 2.1 multiply_subtract_fusion
  314.6 2.5 copy.75
  320.6 2.6 copy.79
  325.8 5.9 all-reduce
  334.0 2.6 fusion.2
  339.3 2.6 fusion.3
  342.0 3.3 fusion.18
  346.2 2.6 fusion.4
  349.0 4.4 convolution_convert_fusion.3
  356.9 2.6 add_convert_fusion
  359.6 10.0 convolution_convert_fusion.2
  370.0 10.0 convolution_convert_fusion.1
  380.1 10.0 convolution_convert_fusion
  393.4 58.1 %reduce-scatter.20.cloned.1.call-done = bf16[256,512]{0,1:T(8,128)(2,1)} async-done(((bf16[2048,512]{0,1:T(8,128)(2,1)}), bf16[256,512]{0,1:T(8,128)(2,1)}) %reduce-scatter.20.cloned.1.call-update) | async-done | bytes 262160 | tf_op jit(solution)/shard_map/reduce_scatter | solution.py:239
  453.5 69.8 %reduce-scatter.22.cloned.1.call-done = bf16[256,512]{0,1:T(8,128)(2,1)} async-done(((bf16[2048,512]{0,1:T(8,128)(2,1)}), bf16[256,512]{0,1:T(8,128)(2,1)}) %reduce-scatter.22.cloned.1.call-update) | async-done | bytes 262160 | tf_op jit(solution)/shard_map/reduce_scatter | solution.py:242
  525.2 69.4 %reduce-scatter.24.cloned.1.call-done = bf16[256,512]{0,1:T(8,128)(2,1)} async-done(((bf16[2048,512]{0,1:T(8,128)(2,1)}), bf16[256,512]{0,1:T(8,128)(2,1)}) %reduce-scatter.24.cloned.1.call-update) | async-done | bytes 262160 | tf_op jit(solution)/shard_map/reduce_scatter | solution.py:245
  596.5 69.1 %reduce-scatter.26.cloned.1.call-done = bf16[512,256]{1,0:T(8,128)(2,1)} async-done(((bf16[512,2048]{1,0:T(8,128)(2,1)}), bf16[512,256]{1,0:T(8,128)(2,1)}) %reduce-scatter.26.cloned.1.call-update) | async-done | bytes 262160 | tf_op jit(solution)/shard_map/reduce_scatter | solution.py:248
  667.4 31.9 %reduce-scatter.18.cloned.1.call-done = bf16[128,2048]{1,0:T(8,128)(2,1)} async-done(((bf16[512,2048]{1,0:T(8,128)(2,1)}), bf16[128,2048]{1,0:T(8,128)(2,1)}) %reduce-scatter.18.cloned.1.call-update) | async-done | bytes 524304 | tf_op jit(solution)/shard_map/reduce_scatter | solution.py:219
  699.3 2.1 add_convert_fusion.2
  701.3 150.5 %reduce-scatter.28.cloned.1.call-done = bf16[256,2048]{1,0:T(8,128)(2,1)} async-done(((bf16[2048,2048]{1,0:T(8,128)(2,1)}), bf16[256,2048]{1,0:T(8,128)(2,1)}) %reduce-scatter.28.cloned.1.call-update) | async-done | bytes 1048592 | tf_op jit(solution)/shard_map/reduce_scatter | solution.py:251
  851.8 2.8 convert_element_type.217
  854.6 149.1 %reduce-scatter.30.cloned.1.call-done = bf16[256,2048]{1,0:T(8,128)(2,1)} async-done(((bf16[2048,2048]{1,0:T(8,128)(2,1)}), bf16[256,2048]{1,0:T(8,128)(2,1)}) %reduce-scatter.30.cloned.1.call-update) | async-done | bytes 1048592 | tf_op jit(solution)/shard_map/reduce_scatter | solution.py:254
  1003.7 2.8 convert_element_type.219
  1006.5 149.1 %reduce-scatter.32.cloned.1.call-done = bf16[2048,256]{1,0:T(8,128)(2,1)} async-done(((bf16[2048,2048]{1,0:T(8,128)(2,1)}), bf16[2048,256]{1,0:T(8,128)(2,1)}) %reduce-scatter.32.cloned.1.call-update) | async-done | bytes 1048592 | tf_op jit(solution)/shard_map/reduce_scatter | solution.py:257
  1155.7 2.7 convert_element_type.221
  (184 shorter events, 59.5 us)
Async XLA Ops:
  7.2 27.7 %copy-start = (bf16[2048,512]{1,0:T(8,128)(2,1)S(1)}, bf16[2048,512]{1,0:T(8,128)(2,1)}, u32[]{:S(2)}) copy-start(bf16[2048,512]{1,0:T(8,128)(2,1)} %param.16) | copy-start | bytes 6291460
  7.2 27.7 %all-gather.8.cloned.1.call-start = ((), (), s32[]{:S(2)}) async-start(), calls=%async_computation.11 | async-start | bytes 2621440 | tf_op jit(solution)/shard_map/all_gather | solution.py:129
  7.9 93.8 %reduce-scatter.12.cloned.1.call-start = ((), (), s32[]{:S(2)}) async-start(), calls=%async_computation.12 | async-start | bytes 2621440 | tf_op jit(solution)/shard_map/reduce_scatter | solution.py:151
  34.9 4.0 copy-start.24
  34.9 4.0 copy-start.35
  38.9 8.1 copy-start.32
  48.5 2.7 copy-start.33
  55.3 2.9 copy-start.26
  59.6 5.1 copy-start.1
  59.6 3.1 copy-start.19
  59.6 3.7 copy-start.36
  64.7 1.8 copy-start.34
  69.1 33.9 %copy-start.5 = (bf16[128,2048]{1,0:T(8,128)(2,1)S(1)}, bf16[128,2048]{1,0:T(8,128)(2,1)}, u32[]{:S(2)}) copy-start(bf16[128,2048]{1,0:T(8,128)(2,1)} %param.14) | copy-start | bytes 1572868
  69.1 33.9 %copy-start.30 = (f32[2048]{0:T(1024)S(1)}, f32[2048]{0:T(1024)}, u32[]{:S(2)}) copy-start(f32[2048]{0:T(1024)} %param.25) | copy-start | bytes 24580
  69.1 58.8 %all-gather.10.cloned.1.call-start = ((), (), s32[]{:S(2)}) async-start(), calls=%async_computation.13 | async-start | bytes 2621440 | tf_op jit(solution)/shard_map/all_gather | solution.py:160
  105.1 81.7 %reduce-scatter.14.cloned.1.call-start = ((), (), s32[]{:S(2)}) async-start(), calls=%async_computation.14 | async-start | bytes 2621440 | tf_op jit(solution)/shard_map/reduce_scatter | solution.py:165
  127.9 8.5 copy-start.40
  127.9 21.6 %slice-start = ((s8[8388608]{0:T(1024)(128)(4,1)}), s8[4194304]{0:T(1024)(128)(4,1)S(1)}, s32[]{:S(2)}) async-start(s8[8388608]{0:T(1024)(128)(4,1)} %bitcast.130), calls=%async_computation.27 | async-start | bytes 8388608
  136.4 11.7 %copy-start.42 = (f32[512,2048]{1,0:T(8,128)}, f32[512,2048]{1,0:T(8,128)S(1)}, u32[]{:S(2)}) copy-start(f32[512,2048]{1,0:T(8,128)S(1)} %fusion.52) | copy-start | bytes 12582916
  136.4 13.1 %slice-start.1 = ((s8[8388608]{0:T(1024)(128)(4,1)}), s8[4194304]{0:T(1024)(128)(4,1)S(1)}, s32[]{:S(2)}) async-start(s8[8388608]{0:T(1024)(128)(4,1)} %bitcast.130), calls=%async_computation.28 | async-start | bytes 8388608
  155.2 32.9 %copy-start.3 = (bf16[128,2048]{1,0:T(8,128)(2,1)S(1)}, bf16[128,2048]{1,0:T(8,128)(2,1)}, u32[]{:S(2)}) copy-start(bf16[128,2048]{1,0:T(8,128)(2,1)} %param.27) | copy-start | bytes 1572868
  155.2 32.9 %copy-start.31 = (f32[2048]{0:T(1024)S(1)}, f32[2048]{0:T(1024)}, u32[]{:S(2)}) copy-start(f32[2048]{0:T(1024)} %param.26) | copy-start | bytes 24580
  155.2 59.3 %all-gather.12.cloned.1.call-start = ((), (), s32[]{:S(2)}) async-start(), calls=%async_computation.15 | async-start | bytes 2621440 | tf_op jit(solution)/shard_map/all_gather | solution.py:176
  191.8 84.0 %reduce-scatter.16.cloned.1.call-start = ((), (), s32[]{:S(2)}) async-start(), calls=%async_computation.16 | async-start | bytes 2621440 | tf_op jit(solution)/shard_map/reduce_scatter | solution.py:185
  226.4 8.5 copy-start.45
  226.4 8.5 copy-start.44
  244.1 31.6 %copy-start.4 = (bf16[128,2048]{1,0:T(8,128)(2,1)S(1)}, bf16[128,2048]{1,0:T(8,128)(2,1)}, u32[]{:S(2)}) copy-start(bf16[128,2048]{1,0:T(8,128)(2,1)} %reduce-scatter.12.cloned.1.call-done) | copy-start | bytes 1572868
  244.1 58.8 %all-gather.14.cloned.1.call-start = ((), (), s32[]{:S(2)}) async-start(), calls=%async_computation.17 | async-start | bytes 2621440 | tf_op jit(solution)/shard_map/all_gather | solution.py:192
  280.2 109.9 %all-gather.16.cloned.1.call-start = ((), (), s32[]{:S(2)}) async-start(), calls=%async_computation.26 | async-start | bytes 1081344 | tf_op jit(solution)/shard_map/all_gather | solution.py:235
  280.5 26.2 %copy-start.29 = (bf16[512,512]{0,1:T(8,128)(2,1)S(1)}, bf16[512,512]{0,1:T(8,128)(2,1)}, u32[]{:S(2)}) copy-start(bf16[512,512]{0,1:T(8,128)(2,1)} %copy-done.28) | copy-start | bytes 1572868
  303.0 3.7 copy-start.2
  317.1 2.0 copy-start.15
  317.1 2.2 copy-start.16
  325.8 125.8 %reduce-scatter.20.cloned.1.call-start = ((), (), s32[]{:S(2)}) async-start(), calls=%async_computation.19 | async-start | bytes 2359296 | tf_op jit(solution)/shard_map/reduce_scatter | solution.py:239
  331.7 2.2 copy-start.37
  336.6 186.7 %reduce-scatter.22.cloned.1.call-start = ((), (), s32[]{:S(2)}) async-start(), calls=%async_computation.20 | async-start | bytes 2359296 | tf_op jit(solution)/shard_map/reduce_scatter | solution.py:242
  336.6 2.7 copy-start.38
  341.9 252.7 %reduce-scatter.24.cloned.1.call-start = ((), (), s32[]{:S(2)}) async-start(), calls=%async_computation.21 | async-start | bytes 2359296 | tf_op jit(solution)/shard_map/reduce_scatter | solution.py:245
  342.0 4.2 copy-start.39
  348.8 316.8 %reduce-scatter.26.cloned.1.call-start = ((), (), s32[]{:S(2)}) async-start(), calls=%async_computation.22 | async-start | bytes 2359296 | tf_op jit(solution)/shard_map/reduce_scatter | solution.py:248
  353.4 345.8 %reduce-scatter.18.cloned.1.call-start = ((), (), s32[]{:S(2)}) async-start(), calls=%async_computation.18 | async-start | bytes 2621440 | tf_op jit(solution)/shard_map/reduce_scatter | solution.py:219
  353.5 1.8 copy-start.25
  355.2 1.6 copy-start.20
  355.2 1.7 copy-start.23
  359.6 492.3 %reduce-scatter.28.cloned.1.call-start = ((), (), s32[]{:S(2)}) async-start(), calls=%async_computation.23 | async-start | bytes 9437184 | tf_op jit(solution)/shard_map/reduce_scatter | solution.py:251
  369.7 634.1 %reduce-scatter.30.cloned.1.call-start = ((), (), s32[]{:S(2)}) async-start(), calls=%async_computation.24 | async-start | bytes 9437184 | tf_op jit(solution)/shard_map/reduce_scatter | solution.py:254
  380.0 775.6 %reduce-scatter.32.cloned.1.call-start = ((), (), s32[]{:S(2)}) async-start(), calls=%async_computation.25 | async-start | bytes 9437184 | tf_op jit(solution)/shard_map/reduce_scatter | solution.py:257
  390.1 309.1 %copy-start.6 = (bf16[128,2048]{1,0:T(8,128)(2,1)S(1)}, bf16[128,2048]{1,0:T(8,128)(2,1)}, u32[]{:S(2)}) copy-start(bf16[128,2048]{1,0:T(8,128)(2,1)} %reduce-scatter.16.cloned.1.call-done) | copy-start | bytes 1572868
  (16 other events, 18.6 us)
Sparse Core Ops, SparseCore 0:
  9.6 25.2 all-gather.7
  69.2 32.5 reduce-scatter.11
  105.3 22.5 all-gather.9
  155.3 31.4 reduce-scatter.13
  191.9 22.5 all-gather.11
  244.3 31.4 reduce-scatter.15
  280.4 22.5 all-gather.13
  325.9 53.6 all-gather.15
  384.1 67.3 reduce-scatter.19
  455.9 67.2 reduce-scatter.21
  527.2 67.3 reduce-scatter.23
  598.4 67.1 reduce-scatter.25
  668.8 30.3 reduce-scatter.17
  702.7 149.0 reduce-scatter.27
  855.7 147.9 reduce-scatter.29
  1007.2 148.3 reduce-scatter.31
